TPU v7x, 512 devices: a whole 4x4x16 slice. The times are simulated.
512 devices in a mesh: rcpt: 8 (over x, core), cell: 64 (over z, y).
Axes of the slice: x: 4, y: 4, z: 16, core: 2. Of those that a mesh axis runs over, the one named last changes fastest.
Arguments:
- footprint: bfloat16 [4096, 131072], P(('rcpt', 'cell')), may hold values from -0.015625 to 0.015625
- prior_draws: bfloat16 [128, 131072], P(None, 'cell'), may hold values from -6 to 6
- observed: float32 [4096], P('rcpt'), may hold values from -6 to 6
- obs_noise: float32 [4096, 128], P('rcpt'), may hold values from -6 to 6
- batch_of: int32 [4096], P('rcpt'), may hold values from 0 to 63
- batch_variance: float32 [64], replicated, may hold values from 0.1 to 2
- band_offsets: int32 [3], replicated, may hold values from 1 to 8, as said below
- center_block: float32 [128, 128], replicated, may hold values from -5 to 6.5, as said below
- band_blocks: float32 [3, 128, 128], replicated, may hold values from -1 to 1, as said below
Outputs:
- post_flux: float32 [128, 131072], P('rcpt', 'cell')
- obs_weights: float32 [4096, 128], P(('rcpt', 'cell'))
Inputs may be any that keep to these rules, and one draw needn't show every extreme that they name: `band_offsets`: the offsets are distinct, and one of them is 8. `center_block`: symmetric; with band_blocks it makes the prior operator positive definite. `band_blocks`: with center_block it makes the prior operator positive definite.
All inputs are finite; a program needn't handle non-finite values.
Results may differ from a plain program's by a relative error of at most 0.0035.
Values may be sent and summed in bfloat16 or wider, within the bound.
A program may use at most 64 MiB of HBM per device.

v0:
```python
import jax
import jax.numpy as jnp
from jax import lax
from jax.sharding import PartitionSpec as P

REACH = 8
ITERS = 2


def extended(block, sides, width):
    for axis, dim in sides:
        count = lax.axis_size(axis)
        forward = [(i, i + 1) for i in range(count - 1)]
        backward = [(target, source) for source, target in forward]
        low = lax.ppermute(
            lax.slice_in_dim(block, block.shape[dim] - width, None, axis=dim), axis, forward
        )
        high = lax.ppermute(lax.slice_in_dim(block, 0, width, axis=dim), axis, backward)
        block = jnp.concatenate([low, block, high], axis=dim)
    return block


def band_sum(field_in, padded, band_offsets, center_block, band_blocks):
    block_width = center_block.shape[0]
    row_count, cell_parts = field_in.shape
    shaped = (row_count, cell_parts // block_width, block_width)
    running = jnp.einsum(
        "rbk,kj->rbj", field_in.reshape(shaped), center_block, precision=lax.Precision.HIGHEST
    )
    for band in range(band_blocks.shape[0]):
        offset = band_offsets[band]
        ahead = lax.dynamic_slice_in_dim(padded, (REACH + offset) * block_width, cell_parts, 1)
        behind = lax.dynamic_slice_in_dim(padded, (REACH - offset) * block_width, cell_parts, 1)
        running = running + jnp.einsum(
            "rbk,kj->rbj", ahead.reshape(shaped), band_blocks[band], precision=lax.Precision.HIGHEST
        )
        running = running + jnp.einsum(
            "rbk,jk->rbj",
            behind.reshape(shaped),
            band_blocks[band],
            precision=lax.Precision.HIGHEST,
        )
    return running.reshape(row_count, cell_parts)


def prior_apply(field_in, band_offsets, center_block, band_blocks):
    margin = REACH * center_block.shape[0]
    padded = extended(field_in.astype(jnp.bfloat16), (("cell", 1),), margin).astype(field_in.dtype)
    return band_sum(field_in, padded, band_offsets, center_block, band_blocks)


def local(
    footprint,
    prior_draws,
    observed,
    obs_noise,
    batch_of,
    batch_variance,
    band_offsets,
    center_block,
    band_blocks,
):
    placed = lax.all_to_all(footprint, "cell", split_axis=1, concat_axis=0, tiled=True)
    share_rows = placed.shape[0] // lax.axis_size("cell")
    row_start = lax.axis_index("cell") * share_rows
    sample_count = obs_noise.shape[1]
    sample_rows = sample_count // lax.axis_size("rcpt")
    sample_start = lax.axis_index("rcpt") * sample_rows
    levels = jnp.arange(batch_variance.shape[0], dtype=jnp.int32)
    matches = (batch_of[:, None] == levels[None, :]).astype(jnp.float32)
    noise_var = jnp.sum(matches * batch_variance[None, :], axis=1)
    contract_rows = (((0,), (0,)), ((), ()))
    contract_cells = (((1,), (1,)), ((), ()))

    def obs_total(partial_sum):
        return lax.psum(partial_sum, "cell")

    def sample_sums(values):
        return lax.psum(values, "rcpt")

    def back_project(vector):
        return lax.dot_general(
            vector.astype(jnp.bfloat16), placed, contract_rows, preferred_element_type=jnp.float32
        )

    def forward(partial_sum):
        summed = lax.psum(partial_sum.astype(jnp.bfloat16), "rcpt").astype(jnp.float32)
        smooth = prior_apply(summed, band_offsets, center_block, band_blocks).astype(jnp.bfloat16)
        return lax.dot_general(placed, smooth, contract_cells, preferred_element_type=jnp.float32)

    base = obs_total(
        lax.dot_general(placed, prior_draws, contract_cells, preferred_element_type=jnp.float32)
    )
    residual = observed[:, None] + jnp.sqrt(noise_var)[:, None] * obs_noise - base
    direction = residual
    weights = jnp.zeros_like(residual)
    norm_now = sample_sums(jnp.sum(residual * residual, axis=0))
    for iteration in range(ITERS):
        applied = obs_total(forward(back_project(direction))) + noise_var[:, None] * direction
        step_size = norm_now / sample_sums(jnp.sum(direction * applied, axis=0))
        weights = weights + step_size[None, :] * direction
        if iteration + 1 < ITERS:
            residual = residual - step_size[None, :] * applied
            norm_next = sample_sums(jnp.sum(residual * residual, axis=0))
            direction = residual + (norm_next / norm_now)[None, :] * direction
            norm_now = norm_next
    owned_terms = lax.psum_scatter(
        back_project(weights).astype(jnp.bfloat16), "rcpt", scatter_dimension=0, tiled=True
    ).astype(jnp.float32)
    own_prior = lax.dynamic_slice_in_dim(prior_draws, sample_start, sample_rows, 0).astype(
        jnp.float32
    )
    posterior = own_prior + prior_apply(owned_terms, band_offsets, center_block, band_blocks)
    return (posterior, lax.dynamic_slice_in_dim(weights, row_start, share_rows, 0))


def solution(mesh):
    return jax.shard_map(
        local,
        mesh=mesh,
        in_specs=(
            P(("rcpt", "cell"), None),
            P(None, "cell"),
            P("rcpt"),
            P("rcpt", None),
            P("rcpt"),
            P(),
            P(),
            P(),
            P(),
        ),
        out_specs=(P("rcpt", "cell"), P(("rcpt", "cell"), None)),
        check_vma=False,
    )
```

profile of v0, /device:TPU:1, one launch (start us, length us, event | category | flops | bytes accessed | tf_op | source)
XLA Modules:
  0.0 1225.0 jit_solution(12135059974696939341)
XLA Ops:
  7.2 114.4 %all_to_all.19 = bf16[8,64,2048]{2,0,1:T(8,128)(2,1)S(1)} all-to-all(bf16[8,64,2048]{2,0,1:T(8,128)(2,1)} %bitcast.187), channel_id=1, replica_groups=mesh['rcpt'=8,'cell'=64] {'cell'}, dimensions={1} | all-to-all | bytes 4194304 | tf_op jit(solution)/shard_map/all_to_all | solution.py:63
  123.3 252.7 %all-reduce.7.cloned.1.call-done = f32[512,128]{1,0:T(8,128)} async-done(((f32[512,128]{1,0:T(8,128)}), f32[512,128]{1,0:T(8,128)}) %all-reduce.7.cloned.1.call-update) | async-done | bytes 262160 | tf_op jit(solution)/shard_map/psum | solution.py:76
  383.1 75.6 %all-reduce.9.cloned.1.call-done = bf16[128,2048]{1,0:T(8,128)(2,1)} async-done(((bf16[128,2048]{1,0:T(8,128)(2,1)}), bf16[128,2048]{1,0:T(8,128)(2,1)}) %all-reduce.9.cloned.1.call-update) | async-done | bytes 524304 | tf_op jit(solution)/shard_map/psum | solution.py:87
  459.8 2.5 collective-permute-start
  463.6 2.6 fusion.20
  466.3 3.1 collective-permute-done.1
  470.9 2.1 copy.79
  475.1 2.1 copy.85
  479.2 2.1 copy.91
  482.3 2.1 convolution_add_fusion.11
  488.9 262.7 %all-reduce.11.cloned.1.call-done = f32[512,128]{1,0:T(8,128)} async-done(((f32[512,128]{1,0:T(8,128)}), f32[512,128]{1,0:T(8,128)}) %all-reduce.11.cloned.1.call-update) | async-done | bytes 262160 | tf_op jit(solution)/shard_map/psum | solution.py:76
  752.7 23.3 %all-reduce = (f32[128]{0:T(128)S(1)}, f32[128]{0:T(128)S(1)}) all-reduce(f32[128]{0:T(128)S(1)} %get-tuple-element.3, f32[128]{0:T(128)S(1)} %get-tuple-element.2), channel_id=1, replica_groups=mesh['rcpt'=8,'cell'=64] {'rcpt'}, use_global_device_ids=true, to_apply=%region_3.0 | all-reduce | flops 256 | bytes 2048 | tf_op jit(solution)/shard_map/psum | solution.py:79
  777.1 12.4 %psum.68 = f32[128]{0:T(128)S(1)} all-reduce(f32[128]{0:T(128)S(1)} %multiply_reduce_fusion.1), channel_id=1, replica_groups=mesh['rcpt'=8,'cell'=64] {'rcpt'}, use_global_device_ids=true, to_apply=%region_9.0 | all-reduce | flops 128 | bytes 1024 | tf_op jit(solution)/shard_map/psum | solution.py:79
  789.5 2.4 convolution_convert_fusion.1
  792.0 67.0 %all-reduce.13.cloned.1.call-done = bf16[128,2048]{1,0:T(8,128)(2,1)} async-done(((bf16[128,2048]{1,0:T(8,128)(2,1)}), bf16[128,2048]{1,0:T(8,128)(2,1)}) %all-reduce.13.cloned.1.call-update) | async-done | bytes 524304 | tf_op jit(solution)/shard_map/psum | solution.py:87
  860.1 2.5 collective-permute-start.2
  864.0 2.6 fusion.17
  866.7 2.9 collective-permute-done.3
  879.4 2.1 copy.110
  882.5 2.1 convolution_add_fusion.5
  889.2 262.7 %all-reduce.15.cloned.1.call-done = f32[512,128]{1,0:T(8,128)} async-done(((f32[512,128]{1,0:T(8,128)}), f32[512,128]{1,0:T(8,128)}) %all-reduce.15.cloned.1.call-update) | async-done | bytes 262160 | tf_op jit(solution)/shard_map/psum | solution.py:76
  1153.0 23.3 %psum.71 = f32[128]{0:T(128)S(1)} all-reduce(f32[128]{0:T(128)S(1)} %multiply_reduce_fusion), channel_id=1, replica_groups=mesh['rcpt'=8,'cell'=64] {'rcpt'}, use_global_device_ids=true, to_apply=%region_13.0 | all-reduce | flops 128 | bytes 1024 | tf_op jit(solution)/shard_map/psum | solution.py:79
  1178.3 29.2 %reduce-scatter.2.cloned.1.call-done = bf16[16,2048]{1,0:T(8,128)(2,1)} async-done(((bf16[128,2048]{1,0:T(8,128)(2,1)}), bf16[16,2048]{1,0:T(8,128)(2,1)}) %reduce-scatter.2.cloned.1.call-update) | async-done | bytes 65552 | tf_op jit(solution)/shard_map/reduce_scatter | solution.py:107
  1208.3 2.1 collective-permute-start.4
  (126 shorter events, 50.1 us)
Async XLA Ops:
  7.2 456.4 %copy-start = (f32[128,128]{1,0:T(8,128)S(1)}, f32[128,128]{1,0:T(8,128)}, u32[]{:S(2)}) copy-start(f32[128,128]{1,0:T(8,128)} %param.16) | copy-start | bytes 196612
  7.2 368.8 %all-reduce.7.cloned.1.call-start = ((), (), s32[]{:S(2)}) async-start(), calls=%async_computation.2 | async-start | bytes 524288 | tf_op jit(solution)/shard_map/psum | solution.py:76
  7.2 114.4 %copy-start.15 = (bf16[128,2048]{1,0:T(8,128)(2,1)S(1)}, bf16[128,2048]{1,0:T(8,128)(2,1)}, u32[]{:S(2)}) copy-start(bf16[128,2048]{1,0:T(8,128)(2,1)} %param.10) | copy-start | bytes 1572868
  121.7 254.3 %copy-start.16 = (f32[512,128]{1,0:T(8,128)S(1)}, f32[512,128]{1,0:T(8,128)}, u32[]{:S(2)}) copy-start(f32[512,128]{1,0:T(8,128)} %param.12) | copy-start | bytes 786436
  121.7 254.3 %copy-start.18 = (f32[512]{0:T(512)S(1)}, f32[512]{0:T(512)}, u32[]{:S(2)}) copy-start(f32[512]{0:T(512)} %param.11) | copy-start | bytes 6148
  123.2 335.5 %all-reduce.9.cloned.1.call-start = ((), (), s32[]{:S(2)}) async-start(), calls=%async_computation.3 | async-start | bytes 1048576 | tf_op jit(solution)/shard_map/psum | solution.py:87
  123.3 255.2 %copy-start.17 = (s32[3]{0:T(128)S(1)}, s32[3]{0:T(128)}, u32[]{:S(2)}) copy-start(s32[3]{0:T(128)} %param.15) | copy-start | bytes 40
  378.5 373.1 %all-reduce.11.cloned.1.call-start = ((), (), s32[]{:S(2)}) async-start(), calls=%async_computation.4 | async-start | bytes 524288 | tf_op jit(solution)/shard_map/psum | solution.py:76
  458.7 7.6 copy-start.3
  459.8 6.4 collective-permute-start
  462.3 7.1 collective-permute-start.1
  475.1 7.2 copy-start.1
  482.3 2.1 copy-start.13
  482.3 2.7 copy-start.11
  488.9 370.1 %all-reduce.13.cloned.1.call-start = ((), (), s32[]{:S(2)}) async-start(), calls=%async_computation.5 | async-start | bytes 1048576 | tf_op jit(solution)/shard_map/psum | solution.py:87
  791.9 359.9 %all-reduce.15.cloned.1.call-start = ((), (), s32[]{:S(2)}) async-start(), calls=%async_computation.6 | async-start | bytes 524288 | tf_op jit(solution)/shard_map/psum | solution.py:76
  858.9 7.7 copy-start.4
  860.1 6.6 collective-permute-start.2
  862.5 7.1 collective-permute-start.3
  882.5 2.7 copy-start.12
  887.7 264.2 %copy-start.2 = (f32[512,128]{1,0:T(8,128)S(1)}, f32[512,128]{1,0:T(8,128)}, u32[]{:S(2)}) copy-start(f32[512,128]{1,0:T(8,128)} %all-reduce.11.cloned.1.call-done) | copy-start | bytes 786436
  889.1 318.4 %reduce-scatter.2.cloned.1.call-start = ((), (), s32[]{:S(2)}) async-start(), calls=%async_computation.7 | async-start | bytes 589824 | tf_op jit(solution)/shard_map/reduce_scatter | solution.py:107
  1208.3 4.5 collective-permute-start.4
  1210.4 4.7 collective-permute-start.5
  (9 other events, 12.5 us)
Sparse Core Ops, SparseCore 0:
  123.3 252.6 all-reduce.6
  378.6 80.0 all-reduce.8
  489.0 262.5 all-reduce.10
  792.0 66.8 all-reduce.12
  889.2 262.5 all-reduce.14
  1177.8 29.6 reduce-scatter.1
where the time goes:
time: 1230 us
  waiting for transfers between devices  957 us (78%)
  blocking collectives  173 us (14%)
  local copies, waits for them, and re-layouts  32 us (3%)
  matrix products  26.1 us (2%)
  between operations  18.6 us (2%)
    psum x3, waiting for transfers between devices, obs_total(): return lax.psum(partial_sum, 'cell')  778 us
    psum x2, waiting for transfers between devices, forward(): lax.psum(partial_sum.astype(jnp.bfloat16), 'rcpt').astype(jnp.float32)  143 us
    all_to_all x1, blocking collectives, local(): lax.all_to_all(footprint, 'cell', split_axis=1, concat_axis=0, tiled=True)  114 us
    psum x3, blocking collectives, sample_sums(): return lax.psum(values, 'rcpt')  59 us
    reduce_scatter x1, waiting for transfers between devices, local(): lax.psum_scatter(back_project(weights).astype(jnp.bfloat16), 'rcpt', scat...  29.2 us
  transfers between devices with their start and end apart: 12, of which 9 were waited for; matrix products, arithmetic and copies ran while one was open for 1% of the time, Pallas kernels for 0%

commit v1 on v0

v1 whole, which is shorter than its diff:
```python
import functools

import jax
import jax.numpy as jnp
from jax import lax
from jax.experimental import pallas as pl
from jax.experimental.pallas import tpu as pltpu
from jax.sharding import PartitionSpec as P

REACH = 8
OWN = 8
LANE = 128
MESH = pl.DeviceIdType.MESH
F32 = jnp.float32
BF16 = jnp.bfloat16


def nt_dot(a, b):
    return lax.dot_general(a, b, (((1,), (1,)), ((), ())), preferred_element_type=F32)


def tn_dot(a, b):
    return lax.dot_general(a, b, (((0,), (0,)), ((), ())), preferred_element_type=F32)


def nn_dot(a, b):
    return lax.dot_general(a, b, (((1,), (0,)), ((), ())), preferred_element_type=F32)


def kernel(
    dims,
    h_ref,
    prior_ref,
    rc_ref,
    nv_ref,
    offsets_ref,
    center_ref,
    bands_ref,
    post_ref,
    weights_ref,
    hbuf,
    hm,
    gath,
    own_prior,
    qp,
    qr,
    vown,
    vb,
    fpart,
    fsend,
    frecv,
    fown,
    fpad,
    smooth,
    sbf,
    resid,
    gvec,
    gplane,
    gsum,
    gz,
    h_sem,
    q_sem,
    v_sem,
    ring_sem,
    f_sem,
    s_sem,
    gp_sem,
    gz_sem,
    loc_sem,
):
    n_r, n_z, n_y, bpp, samples = dims
    n_plane = n_r * n_y
    n_cell = n_z * n_y
    n_half = REACH // bpp
    n_blocks = n_r * bpp
    s_rows = samples // n_r
    hb = bpp // 2
    rows = n_plane * OWN
    xc = lax.axis_index("rcpt")
    cell = lax.axis_index("cell")
    z = lax.div(cell, n_y)
    y = lax.rem(cell, n_y)
    me = xc * n_y + y

    def plane_dev(k):
        p = lax.rem(me + k, n_plane)
        return p, lax.div(p, n_y), lax.rem(p, n_y)

    def z_dev(k):
        zz = lax.rem(z + k + n_z, n_z)
        return zz, (xc, zz * n_y + y)

    def remote(src, dst, send, recv, dev):
        return pltpu.make_async_remote_copy(
            src_ref=src, dst_ref=dst, send_sem=send, recv_sem=recv, device_id=dev, device_id_type=MESH
        )

    def wait_bytes(ref, sem):
        pltpu.make_async_copy(ref, ref, sem).wait()

    local_h = pltpu.make_async_copy(h_ref.at[:, y, xc], hbuf.at[:, me], loc_sem.at[0])
    local_h.start()
    local_p = pltpu.make_async_copy(
        prior_ref.at[pl.ds(pl.multiple_of(xc * s_rows, s_rows), s_rows), :], own_prior, loc_sem.at[1]
    )
    local_p.start()
    pieces = []
    for b in range(bpp):
        column = pl.multiple_of((xc * bpp + b) * LANE, LANE)
        piece = pltpu.make_async_copy(
            prior_ref.at[:, pl.ds(column, LANE)], gath.at[0, z, b], loc_sem.at[2 + b]
        )
        piece.start()
        pieces.append(piece)

    barrier = pltpu.get_barrier_semaphore()

    def greet_plane(k, c):
        _, xx, yy = plane_dev(k)
        pl.semaphore_signal(barrier, inc=1, device_id=(xx, z * n_y + yy), device_id_type=MESH)
        return c

    lax.fori_loop(1, n_plane, greet_plane, 0)

    def greet_z(k, c):
        _, dev = z_dev(k)
        pl.semaphore_signal(barrier, inc=1, device_id=dev, device_id_type=MESH)
        return c

    lax.fori_loop(1, n_z, greet_z, 0)
    edge_lo = (y == 0) & (z > 0)
    edge_hi = (y == n_y - 1) & (z < n_z - 1)

    @pl.when(edge_lo)
    def _():
        def greet(k, c):
            pl.semaphore_signal(barrier, inc=1, device_id=(k, cell - 1), device_id_type=MESH)
            return c

        lax.fori_loop(0, n_r, greet, 0)

    @pl.when(edge_hi)
    def _():
        def greet(k, c):
            pl.semaphore_signal(barrier, inc=1, device_id=(k, cell + 1), device_id_type=MESH)
            return c

        lax.fori_loop(0, n_r, greet, 0)

    greeted = n_plane - 1 + n_z - 1

    @pl.when(edge_lo | edge_hi)
    def _():
        pl.semaphore_wait(barrier, greeted + n_r)

    @pl.when(jnp.logical_not(edge_lo | edge_hi))
    def _():
        pl.semaphore_wait(barrier, greeted)

    def send_h(k, c):
        _, xx, yy = plane_dev(k)
        remote(
            h_ref.at[:, yy, xx], hbuf.at[:, me], h_sem.at[0], h_sem.at[1], (xx, z * n_y + yy)
        ).start()
        return c

    lax.fori_loop(1, n_plane, send_h, 0)
    for piece in pieces:
        piece.wait()

    chains = (
        (0, 1, n_z // 2),
        (0, -1, n_z - 1 - n_z // 2),
        (1, 1, n_z - 1 - n_z // 2),
        (1, -1, n_z // 2),
    )
    short = n_z - 1 - n_z // 2

    def ring(step_fn):
        for ci, chain in enumerate(chains):
            if chain[2] > 0:
                step_fn(ci, chain, 0, True)

        def body(s, c):
            for ci, chain in enumerate(chains):
                step_fn(ci, chain, s, False)
            return c

        lax.fori_loop(1, short, body, 0)
        for s in range(max(short, 1), n_z // 2):
            for ci, chain in enumerate(chains):
                if s < chain[2]:
                    step_fn(ci, chain, s, False)

    def gather_ring(call):
        def copy(ci, chain, s):
            half, sign, _ = chain
            origin = lax.rem(z - sign * s + n_z, n_z)
            _, dev = z_dev(sign)
            part = gath.at[call, origin, pl.ds(half * hb, hb)]
            return remote(part, part, ring_sem.at[call, 0, ci, s], ring_sem.at[call, 1, ci, s], dev)

        def step(ci, chain, s, first):
            if not first:
                copy(ci, chain, s - 1).wait_recv()
            copy(ci, chain, s).start()

        ring(step)
        for ci, chain in enumerate(chains):
            if chain[2] > 0:
                copy(ci, chain, chain[2] - 1).wait_recv()

        def drain(s, c):
            for ci, chain in enumerate(chains):
                copy(ci, chain, s).wait_send()
            return c

        lax.fori_loop(0, short, drain, 0)
        for s in range(short, n_z // 2):
            for ci, chain in enumerate(chains):
                if s < chain[2]:
                    copy(ci, chain, s).wait_send()

    def reduce_ring(call):
        def copy(ci, chain, s):
            _, dev = z_dev(chain[1])
            return remote(
                fsend.at[call, ci, s],
                frecv.at[call, ci, s],
                ring_sem.at[2 + call, 0, ci, s],
                ring_sem.at[2 + call, 1, ci, s],
                dev,
            )

        def step(ci, chain, s, first):
            half, sign, steps = chain
            target = lax.rem(z + sign * (steps - s) + n_z, n_z)
            value = fpart[target, pl.ds(half * hb, hb)]
            if not first:
                copy(ci, chain, s - 1).wait_recv()
                value = value + frecv[call, ci, s - 1].astype(F32)
            fsend[call, ci, s] = value.astype(BF16)
            copy(ci, chain, s).start()

        ring(step)
        for ci, chain in enumerate(chains):
            if chain[2] > 0:
                copy(ci, chain, chain[2] - 1).wait_recv()
        for half in range(2):
            total = fpart[z, pl.ds(half * hb, hb)]
            for ci, chain in enumerate(chains):
                if chain[0] == half and chain[2] > 0:
                    total = total + frecv[call, ci, chain[2] - 1].astype(F32)
            fown[call, pl.ds(half * hb, hb)] = total.astype(BF16)

        def drain(s, c):
            for ci, chain in enumerate(chains):
                copy(ci, chain, s).wait_send()
            return c

        lax.fori_loop(0, short, drain, 0)
        for s in range(short, n_z // 2):
            for ci, chain in enumerate(chains):
                if s < chain[2]:
                    copy(ci, chain, s).wait_send()

    def forward_sum(call):
        def body(k, acc):
            hz = hm[k]
            for b in range(bpp):
                acc = acc + nt_dot(hz[:, b * LANE : (b + 1) * LANE], gath[call, k, b])
            return acc

        acc = lax.fori_loop(0, n_z, body, jnp.zeros((rows, samples), F32))
        qp[call] = acc.reshape(n_plane, OWN, samples)

        def send(k, c):
            p, xx, yy = plane_dev(k)
            remote(
                qp.at[call, p], qr.at[call, me], q_sem.at[call, 0], q_sem.at[call, 1], (xx, z * n_y + yy)
            ).start()
            return c

        lax.fori_loop(1, n_plane, send, 0)
        qr[call, me] = qp[call, me]
        wait_bytes(qr.at[call, pl.ds(0, n_plane - 1)], q_sem.at[call, 1])
        total = jnp.sum(qr[call], axis=0)
        wait_bytes(qp.at[call, pl.ds(0, n_plane - 1)], q_sem.at[call, 0])
        return total

    def share_start(call, value):
        vown[call] = value.astype(BF16)
        vb[call, me] = value.astype(BF16)

        def send(k, c):
            _, xx, yy = plane_dev(k)
            remote(
                vown.at[call], vb.at[call, me], v_sem.at[call, 0], v_sem.at[call, 1], (xx, z * n_y + yy)
            ).start()
            return c

        lax.fori_loop(1, n_plane, send, 0)

    def back(call):
        wait_bytes(vb.at[call, pl.ds(0, n_plane - 1)], v_sem.at[call, 1])
        vector = vb[call].astype(F32).reshape(rows, samples).astype(BF16)

        def body(k, c):
            product = tn_dot(vector, hm[k])
            for b in range(bpp):
                fpart[k, b] = product[:, b * LANE : (b + 1) * LANE]
            return c

        lax.fori_loop(0, n_z, body, 0)
        wait_bytes(vb.at[call, pl.ds(0, n_plane - 1)], v_sem.at[call, 0])

    def spread_field(call):
        @pl.when(cell == 0)
        def _():
            fpad[call, pl.ds(0, REACH)] = jnp.zeros((REACH, s_rows, LANE), BF16)

        @pl.when(cell == n_cell - 1)
        def _():
            fpad[call, pl.ds(REACH + n_blocks, REACH)] = jnp.zeros((REACH, s_rows, LANE), BF16)

        def part(r):
            return fown.at[call, :, pl.ds(pl.multiple_of(r * s_rows, s_rows), s_rows)]

        def send(k, c):
            r = lax.rem(xc + k, n_r)
            remote(
                part(r),
                fpad.at[call, pl.ds(REACH + xc * bpp, bpp)],
                f_sem.at[call, 0],
                f_sem.at[call, 1],
                (r, cell),
            ).start()
            return c

        lax.fori_loop(1, n_r, send, 0)
        low = xc < n_half

        @pl.when(low & (cell > 0))
        def _():
            def send_low(k, c):
                r = lax.rem(xc + k, n_r)
                remote(
                    part(r),
                    fpad.at[call, pl.ds(REACH + n_blocks + xc * bpp, bpp)],
                    f_sem.at[call, 2],
                    f_sem.at[call, 3],
                    (r, cell - 1),
                ).start()
                return c

            lax.fori_loop(0, n_r, send_low, 0)

        @pl.when((xc >= n_r - n_half) & (cell < n_cell - 1))
        def _():
            def send_high(k, c):
                r = lax.rem(xc + k, n_r)
                remote(
                    part(r),
                    fpad.at[call, pl.ds((xc - (n_r - n_half)) * bpp, bpp)],
                    f_sem.at[call, 4],
                    f_sem.at[call, 5],
                    (r, cell + 1),
                ).start()
                return c

            lax.fori_loop(0, n_r, send_high, 0)

        own = pltpu.make_async_copy(
            part(xc), fpad.at[call, pl.ds(REACH + xc * bpp, bpp)], loc_sem.at[2 + bpp + call]
        )
        own.start()
        own.wait()
        body = fpad.at[call, pl.ds(0, (n_r - 1) * bpp)]
        halo = fpad.at[call, pl.ds(0, REACH)]
        wide = fpad.at[call, pl.ds(0, n_blocks)]
        wait_bytes(body, f_sem.at[call, 1])

        @pl.when(cell < n_cell - 1)
        def _():
            wait_bytes(halo, f_sem.at[call, 3])

        @pl.when(cell > 0)
        def _():
            wait_bytes(halo, f_sem.at[call, 5])

        wait_bytes(body, f_sem.at[call, 0])

        @pl.when(low & (cell > 0))
        def _():
            wait_bytes(wide, f_sem.at[call, 2])

        @pl.when((xc >= n_r - n_half) & (cell < n_cell - 1))
        def _():
            wait_bytes(wide, f_sem.at[call, 4])

    def split(matrix):
        high = matrix.astype(BF16)
        return high, (matrix - high.astype(F32)).astype(BF16)

    def prior_apply(call):
        flat = (n_blocks * s_rows, LANE)
        high, low = split(center_ref[...])
        here = fpad[call, pl.ds(REACH, n_blocks)].reshape(flat)
        acc = nn_dot(here, high) + nn_dot(here, low)
        for band in range(bands_ref.shape[0]):
            offset = offsets_ref[band]
            high, low = split(bands_ref[band])
            ahead = fpad[call, pl.ds(REACH + offset, n_blocks)].reshape(flat)
            acc = acc + nn_dot(ahead, high) + nn_dot(ahead, low)
            behind = fpad[call, pl.ds(REACH - offset, n_blocks)].reshape(flat)
            acc = acc + nt_dot(behind, high) + nt_dot(behind, low)
        smooth[call] = acc.reshape(n_blocks, s_rows, LANE)

    row_id = lax.broadcasted_iota(jnp.int32, (s_rows, samples), 0)
    lane_id = lax.broadcasted_iota(jnp.int32, (s_rows, samples), 1)
    own_lane = lane_id == row_id + xc * s_rows

    def to_lanes(column):
        return jnp.sum(jnp.where(own_lane, column, 0.0), axis=0, keepdims=True)

    def to_column(lanes):
        return jnp.sum(jnp.where(own_lane, lanes, 0.0), axis=1, keepdims=True)

    def field_dot(field, image):
        return to_lanes(jnp.sum(jnp.sum(field * image, axis=0), axis=1, keepdims=True))

    def row_dot(a, b):
        return jnp.sum(a * b, axis=0, keepdims=True)

    def total_start(call, first, second):
        gvec[call] = jnp.concatenate(
            [first, second, jnp.zeros((OWN - 2, samples), F32)], axis=0
        )

        def send(k, c):
            _, xx, yy = plane_dev(k)
            remote(
                gvec.at[call],
                gplane.at[call, me],
                gp_sem.at[call, 0],
                gp_sem.at[call, 1],
                (xx, z * n_y + yy),
            ).start()
            return c

        lax.fori_loop(1, n_plane, send, 0)
        gplane[call, me] = gvec[call]

    def total_middle(call):
        wait_bytes(gplane.at[call, pl.ds(0, n_plane - 1)], gp_sem.at[call, 1])
        gsum[call] = jnp.sum(gplane[call], axis=0)

        def send(k, c):
            _, dev = z_dev(k)
            remote(
                gsum.at[call], gz.at[call, z], gz_sem.at[call, 0], gz_sem.at[call, 1], dev
            ).start()
            return c

        lax.fori_loop(1, n_z, send, 0)
        gz[call, z] = gsum[call]
        wait_bytes(gplane.at[call, pl.ds(0, n_plane - 1)], gp_sem.at[call, 0])

    def total_end(call):
        wait_bytes(gz.at[call, pl.ds(0, n_z - 1)], gz_sem.at[call, 1])
        total = jnp.sum(gz[call], axis=0)
        wait_bytes(gz.at[call, pl.ds(0, n_z - 1)], gz_sem.at[call, 0])
        return total[0:1], total[1:2]

    gather_ring(0)
    local_h.wait()
    wait_bytes(hbuf.at[:, pl.ds(0, n_plane - 1)], h_sem.at[1])

    def relayout(k, c):
        hm[k] = hbuf[k].astype(F32).reshape(rows, bpp * LANE).astype(BF16)
        return c

    lax.fori_loop(0, n_z, relayout, 0)

    first = rc_ref[...] - forward_sum(0)
    resid[0] = first
    share_start(0, first)
    back(0)
    reduce_ring(0)
    spread_field(0)
    prior_apply(0)

    sbf[...] = smooth[0].astype(BF16)

    def smooth_dst():
        return gath.at[1, z, :, pl.ds(pl.multiple_of(xc * s_rows, s_rows), s_rows)]

    def send_smooth(k, c):
        r = lax.rem(xc + k, n_r)
        remote(
            sbf.at[pl.ds(r * bpp, bpp)], smooth_dst(), s_sem.at[0], s_sem.at[1], (r, cell)
        ).start()
        return c

    lax.fori_loop(1, n_r, send_smooth, 0)
    keep = pltpu.make_async_copy(sbf.at[pl.ds(xc * bpp, bpp)], smooth_dst(), loc_sem.at[4 + bpp])
    keep.start()
    r0 = resid[0]
    energy = field_dot(fpad[0, pl.ds(REACH, n_blocks)].astype(F32), smooth[0])
    total_start(0, row_dot(r0, r0), energy + row_dot(r0 * nv_ref[...], r0))
    keep.wait()
    others = sbf.at[pl.ds(0, (n_r - 1) * bpp)]
    wait_bytes(others, s_sem.at[1])
    gather_ring(1)
    total_middle(0)
    applied = forward_sum(1) + nv_ref[...] * resid[0]
    wait_bytes(others, s_sem.at[0])
    norm0, curve0 = total_end(0)
    alpha0 = norm0 / curve0
    second = resid[0] - alpha0 * applied
    resid[1] = second
    share_start(1, second)
    total_start(1, row_dot(second, second), jnp.zeros((1, samples), F32))
    back(1)
    total_middle(1)
    reduce_ring(1)
    spread_field(1)
    prior_apply(1)
    norm1, _ = total_end(1)
    beta = norm1 / norm0
    direction = resid[1] + beta * resid[0]
    beta_column = to_column(beta)
    field0 = fpad[0, pl.ds(REACH, n_blocks)].astype(F32)
    field1 = fpad[1, pl.ds(REACH, n_blocks)].astype(F32)
    energy = field_dot(field1 + beta_column * field0, smooth[1] + beta_column * smooth[0])
    total_start(2, energy + row_dot(direction * nv_ref[...], direction), jnp.zeros((1, samples), F32))
    total_middle(2)
    local_p.wait()
    curve1, _ = total_end(2)
    alpha1 = norm1 / curve1
    weights_ref[...] = alpha0 * resid[0] + alpha1 * direction
    scale0 = to_column(alpha0 + alpha1 * beta)
    scale1 = to_column(alpha1)
    for b in range(n_blocks):
        columns = slice(b * LANE, (b + 1) * LANE)
        post_ref[:, columns] = (
            own_prior[:, columns].astype(F32) + scale0 * smooth[0, b] + scale1 * smooth[1, b]
        )
    wait_bytes(hbuf.at[:, pl.ds(0, n_plane - 1)], h_sem.at[0])


def local(
    n_r,
    n_z,
    n_y,
    footprint,
    prior_draws,
    observed,
    obs_noise,
    batch_of,
    batch_variance,
    band_offsets,
    center_block,
    band_blocks,
):
    samples = obs_noise.shape[1]
    n_blocks = prior_draws.shape[1] // LANE
    bpp = n_blocks // n_r
    n_plane = n_r * n_y
    s_rows = samples // n_r
    width = bpp * LANE
    rows = n_plane * OWN
    hb = bpp // 2
    steps = n_z // 2
    start = lax.axis_index("cell") * OWN
    levels = jnp.arange(batch_variance.shape[0], dtype=jnp.int32)
    own_batch = lax.dynamic_slice_in_dim(batch_of, start, OWN, 0)
    own_observed = lax.dynamic_slice_in_dim(observed, start, OWN, 0)
    own_noise = lax.dynamic_slice_in_dim(obs_noise, start, OWN, 0)
    matches = (own_batch[:, None] == levels[None, :]).astype(F32)
    noise_var = jnp.sum(matches * batch_variance[None, :], axis=1)
    target = own_observed[:, None] + jnp.sqrt(noise_var)[:, None] * own_noise
    noise_wide = jnp.broadcast_to(noise_var[:, None], (OWN, samples))
    tiles = footprint.reshape(OWN, n_z, n_y, n_r, width).transpose(1, 2, 3, 0, 4)
    vmem = pl.BlockSpec(memory_space=pltpu.VMEM)
    hbm = pl.BlockSpec(memory_space=pl.ANY)
    dma = pltpu.SemaphoreType.DMA
    return pl.pallas_call(
        functools.partial(kernel, (n_r, n_z, n_y, bpp, samples)),
        out_shape=(
            jax.ShapeDtypeStruct((s_rows, n_blocks * LANE), F32),
            jax.ShapeDtypeStruct((OWN, samples), F32),
        ),
        in_specs=[hbm, hbm, vmem, vmem, pl.BlockSpec(memory_space=pltpu.SMEM), vmem, vmem],
        out_specs=(vmem, vmem),
        scratch_shapes=[
            pltpu.VMEM((n_z, n_plane, OWN, width), BF16),
            pltpu.VMEM((n_z, rows, width), BF16),
            pltpu.VMEM((2, n_z, bpp, samples, LANE), BF16),
            pltpu.VMEM((s_rows, n_blocks * LANE), BF16),
            pltpu.VMEM((2, n_plane, OWN, samples), F32),
            pltpu.VMEM((2, n_plane, OWN, samples), F32),
            pltpu.VMEM((2, OWN, samples), BF16),
            pltpu.VMEM((2, n_plane, OWN, samples), BF16),
            pltpu.VMEM((n_z, bpp, samples, LANE), F32),
            pltpu.VMEM((2, 4, steps, hb, samples, LANE), BF16),
            pltpu.VMEM((2, 4, steps, hb, samples, LANE), BF16),
            pltpu.VMEM((2, bpp, samples, LANE), BF16),
            pltpu.VMEM((2, n_blocks + 2 * REACH, s_rows, LANE), BF16),
            pltpu.VMEM((2, n_blocks, s_rows, LANE), F32),
            pltpu.VMEM((n_blocks, s_rows, LANE), BF16),
            pltpu.VMEM((2, OWN, samples), F32),
            pltpu.VMEM((3, OWN, samples), F32),
            pltpu.VMEM((3, n_plane, OWN, samples), F32),
            pltpu.VMEM((3, OWN, samples), F32),
            pltpu.VMEM((3, n_z, OWN, samples), F32),
            dma((2,)),
            dma((2, 2)),
            dma((2, 2)),
            dma((4, 2, 4, steps)),
            dma((2, 6)),
            dma((2,)),
            dma((3, 2)),
            dma((3, 2)),
            dma((5 + bpp,)),
        ],
        compiler_params=pltpu.CompilerParams(
            collective_id=0, has_side_effects=True, vmem_limit_bytes=56 * 1024 * 1024
        ),
    )(tiles, prior_draws, target, noise_wide, band_offsets, center_block, band_blocks)


def solution(mesh, n_y=4):
    n_r = mesh.shape["rcpt"]
    n_z = mesh.shape["cell"] // n_y
    return jax.shard_map(
        functools.partial(local, n_r, n_z, n_y),
        mesh=mesh,
        in_specs=(
            P(("rcpt", "cell"), None),
            P(None, "cell"),
            P("rcpt"),
            P("rcpt", None),
            P("rcpt"),
            P(),
            P(),
            P(),
            P(),
        ),
        out_specs=(P("rcpt", "cell"), P(("rcpt", "cell"), None)),
        check_vma=False,
    )
```

time: 1230 us -> 204 us (0.17)
  waiting for transfers between devices: 957 us -> 0 us
  Pallas kernels: 0 us -> 196 us
  blocking collectives: 173 us -> 0 us
  local copies, waits for them, and re-layouts: 32 us -> 5.01 us
  matrix products: 26.1 us -> 0 us
  between operations: 18.6 us -> 0.65 us
    psum x5 -> x0, waiting for transfers between devices: 921 us -> none  [the longest x3 778 us: obs_total(): return lax.psum(partial_sum, 'cell')]
    pallas_call x0 -> x1, Pallas kernels: none -> 196 us  [local(): pl.pallas_call(functools.partial(kernel, (n_r, n_z, n_y, bpp, samples)),...]
    all_to_all x1 -> x0, blocking collectives: 114 us -> none  [local(): lax.all_to_all(footprint, 'cell', split_axis=1, concat_axis=0, tiled=True)]
    psum x3 -> x0, blocking collectives: 59 us -> none  [sample_sums(): return lax.psum(values, 'rcpt')]
    reduce_scatter x1 -> x0, waiting for transfers between devices: 29.2 us -> none  [local(): lax.psum_scatter(back_project(weights).astype(jnp.bfloat16), 'rcpt', scat...]
    dot_general x27 -> x0, matrix products: 26.1 us -> none  [the longest x9 7.27 us: band_sum(): jnp.einsum('rbk,kj->rbj', ahead.reshape(shaped), band_blocks[band], preci...]
    dynamic_slice x15 -> x2, local copies, waits for them, and re-layouts: 26.3 us -> 1.51 us  [the longest x1 0.76 us: local(): own_observed = lax.dynamic_slice_in_dim(observed, start, OWN, 0)]
  transfers between devices with their start and end apart: 12 -> 0, of which waited for: 9 -> 0; matrix products, arithmetic and copies ran while one was open for 1% -> 0% of each run, Pallas kernels for 0% -> 0%
where the time goes in v1:
time: 204 us; the launch traced here: 203 us
  Pallas kernels  196 us (96%)
  local copies, waits for them, and re-layouts  5.01 us (2%)
  other arithmetic  2.19 us (1%)
    pallas_call x1, Pallas kernels, local(): pl.pallas_call(functools.partial(kernel, (n_r, n_z, n_y, bpp, samples)),...  196 us

profile of v1, /device:TPU:1, one launch (start us, length us, event | category | flops | bytes accessed | tf_op | source)
XLA Modules:
  0.0 203.4 jit_solution(3162290579126459817)
XLA Ops:
  0.6 0.8 dynamic_slice.9
  1.4 0.8 dynamic_slice.10
  2.1 0.8 select_reduce_fusion
  3.0 1.4 multiply_add_fusion.rc_ref
  4.3 0.7 broadcast_in_dim.2.nv_ref
  5.0 195.6 %shard_map.104 = (f32[16,2048]{1,0:T(8,128)}, f32[8,128]{1,0:T(8,128)}) custom-call(bf16[16,4,8,8,256]{4,3,2,1,0:T(8,128)(2,1)} %bitcast.3, bf16[128,2048]{1,0:T(8,128)(2,1)} %prior_ref.1, f32[8,128]{1,0:T(8,128)} %multiply_add_fusion.rc_ref, f32[8,128]{1,0:T(8,128)} %broadcast_in_dim.2.nv_ref, s32[3]{0:T(128)} %offsets_ref.1, f32[128,128]{1,0:T(8,128)} %center_ref.1, ...), custom_call_target="tpu_custom_call" | custom-call | tf_op jit(solution)/shard_map/pallas_call | solution.py:588
  200.6 1.6 copy.13
  202.2 1.3 copy.14
  (1 shorter events, 0.0 us)

commit v2 on v1

v2 whole, which is shorter than its diff:
```python
import functools

import jax
import jax.numpy as jnp
from jax import lax
from jax.experimental import pallas as pl
from jax.experimental.pallas import tpu as pltpu
from jax.sharding import PartitionSpec as P

REACH = 8
SPLIT = 1
LOW = 2
STRIDE = 13
OWN = 8
LANE = 128
MESH = pl.DeviceIdType.MESH
F32 = jnp.float32
BF16 = jnp.bfloat16


def nt_dot(a, b):
    return lax.dot_general(a, b, (((1,), (1,)), ((), ())), preferred_element_type=F32)


def tn_dot(a, b):
    return lax.dot_general(a, b, (((0,), (0,)), ((), ())), preferred_element_type=F32)


def nn_dot(a, b):
    return lax.dot_general(a, b, (((1,), (0,)), ((), ())), preferred_element_type=F32)


def kernel(
    dims,
    h_ref,
    prior_ref,
    observed_hbm,
    noise_hbm,
    batch_hbm,
    variance_hbm,
    offsets_ref,
    center_hbm,
    bands_hbm,
    post_ref,
    weights_ref,
    hbuf,
    hm,
    gath,
    own_prior,
    qp,
    qr,
    vown,
    vb,
    fpart,
    fsend,
    frecv,
    fown,
    fpad,
    smooth,
    sbf,
    resid,
    gvec,
    gplane,
    gsum,
    gz,
    qacc,
    observed_ref,
    noise_ref,
    batch_ref,
    variance_ref,
    center_ref,
    bands_ref,
    h_sem,
    q_sem,
    v_sem,
    ring_sem,
    f_sem,
    s_sem,
    gp_sem,
    gz_sem,
    loc_sem,
):
    n_r, n_z, n_y, n_low, bpp, samples = dims
    n_plane = n_r * n_y * n_low
    n_cell = n_z * n_low * n_y
    n_half = REACH // bpp
    n_blocks = n_r * bpp
    s_rows = samples // n_r
    hb = bpp // 2
    rows = n_plane * OWN
    xc = lax.axis_index("rcpt")
    cell = lax.axis_index("cell")
    near = n_y * n_low
    z = lax.div(cell, near)
    within = lax.rem(cell, near)
    me = xc * near + within

    def plane_dev(i):
        p = lax.rem(me + i * STRIDE, n_plane)
        xx, low = lax.div(p, near), lax.rem(p, near)
        return p, xx, low, (xx, z * near + low)

    def z_dev(k):
        zz = lax.rem(z + k + n_z, n_z)
        return zz, (xc, zz * near + within)

    def remote(src, dst, send, recv, dev):
        return pltpu.make_async_remote_copy(
            src_ref=src, dst_ref=dst, send_sem=send, recv_sem=recv, device_id=dev, device_id_type=MESH
        )

    def wait_bytes(ref, sem):
        pltpu.make_async_copy(ref, ref, sem).wait()

    local_h = pltpu.make_async_copy(h_ref.at[:, within, xc], hbuf.at[:, me], loc_sem.at[0])
    local_p = pltpu.make_async_copy(
        prior_ref.at[pl.ds(pl.multiple_of(xc * s_rows, s_rows), s_rows), :], own_prior, loc_sem.at[1]
    )
    pieces = []
    for b in range(bpp):
        column = pl.multiple_of((xc * bpp + b) * LANE, LANE)
        piece = pltpu.make_async_copy(
            prior_ref.at[:, pl.ds(column, LANE)], gath.at[0, z, b], loc_sem.at[2 + b]
        )
        piece.start()
        pieces.append(piece)

    barrier = pltpu.get_barrier_semaphore()

    def greet_plane(k, c):
        pl.semaphore_signal(barrier, inc=1, device_id=plane_dev(k)[3], device_id_type=MESH)
        return c

    lax.fori_loop(1, n_plane, greet_plane, 0)

    for sign in (1, -1):
        pl.semaphore_signal(barrier, inc=1, device_id=z_dev(sign)[1], device_id_type=MESH)
    edge_lo = (within == 0) & (z > 0)
    edge_hi = (within == near - 1) & (z < n_z - 1)

    @pl.when(edge_lo)
    def _():
        def greet(k, c):
            pl.semaphore_signal(barrier, inc=1, device_id=(k, cell - 1), device_id_type=MESH)
            return c

        lax.fori_loop(0, n_r, greet, 0)

    @pl.when(edge_hi)
    def _():
        def greet(k, c):
            pl.semaphore_signal(barrier, inc=1, device_id=(k, cell + 1), device_id_type=MESH)
            return c

        lax.fori_loop(0, n_r, greet, 0)

    greeted = n_plane - 1 + 2

    @pl.when(edge_lo | edge_hi)
    def _():
        pl.semaphore_wait(barrier, greeted + n_r)

    @pl.when(jnp.logical_not(edge_lo | edge_hi))
    def _():
        pl.semaphore_wait(barrier, greeted)

    flat = n_r * n_y
    level = lax.div(within, n_y)
    mine = xc * n_y + lax.rem(within, n_y)

    def send_h(i, hop):
        t = lax.rem(mine + i * STRIDE, flat)
        xx = lax.div(t, n_y)
        low = lax.rem(level + hop, n_low) * n_y + lax.rem(t, n_y)
        remote(
            h_ref.at[:, low, xx], hbuf.at[:, me], h_sem.at[0], h_sem.at[1], (xx, z * near + low)
        ).start()

    def send_same(i, c):
        send_h(i, 0)
        return c

    lax.fori_loop(1, flat, send_same, 0)
    batch = flat * (n_low - 1) // (n_z // 2)

    def send_batch(s):
        def body(i, c):
            send_h(lax.rem(i, flat), 1 + lax.div(i, flat))
            return c

        lax.fori_loop(s * batch, (s + 1) * batch, body, 0)

    local_h.start()
    local_p.start()
    loads = [
        pltpu.make_async_copy(src, dst, loc_sem.at[5 + bpp + i])
        for i, (src, dst) in enumerate(
            (
                (observed_hbm, observed_ref),
                (noise_hbm.at[pl.ds(pl.multiple_of(cell * OWN, OWN), OWN), :], noise_ref),
                (batch_hbm, batch_ref),
                (variance_hbm, variance_ref),
                (center_hbm, center_ref),
                (bands_hbm, bands_ref),
            )
        )
    ]
    for load in loads:
        load.start()
    for piece in pieces:
        piece.wait()

    steps = n_z // 2
    short = n_z - 1 - steps
    middle = max(1, short // 2 + 1)
    sub = samples // SPLIT
    chains = []
    for part in range(SPLIT):
        for half, sign, count in ((0, 1, steps), (0, -1, short), (1, 1, short), (1, -1, steps)):
            chains.append((half, part, sign, count))

    def rotate(k):
        return lax.rem(z + k + n_z, n_z)

    def ring(step_fn, after_step, hook_first, hook_middle):
        for ci, chain in enumerate(chains):
            if chain[3] > 0:
                step_fn(ci, chain, 0, True)
        after_step(0)
        hook_first()

        def body(s, c):
            for ci, chain in enumerate(chains):
                step_fn(ci, chain, s, False)
            after_step(s)
            return c

        lax.fori_loop(1, middle, body, 0)
        hook_middle()
        lax.fori_loop(middle, short, body, 0)
        for s in range(max(short, 1), steps):
            for ci, chain in enumerate(chains):
                if s < chain[3]:
                    step_fn(ci, chain, s, False)
                else:
                    step_fn(ci, chain, s, None)
            after_step(s)

    def drain(copy):
        def body(s, c):
            for ci, chain in enumerate(chains):
                copy(ci, chain, s).wait_send()
            return c

        lax.fori_loop(0, short, body, 0)
        for s in range(short, steps):
            for ci, chain in enumerate(chains):
                if s < chain[3]:
                    copy(ci, chain, s).wait_send()

    def gather_copy(call, ci, chain, s):
        half, part, sign, _ = chain
        origin = rotate(-sign * s)
        piece = gath.at[
            call, origin, pl.ds(half * hb, hb), pl.ds(part * sub, sub)
        ]
        return remote(
            piece, piece, ring_sem.at[call, 0, ci, s], ring_sem.at[call, 1, ci, s], z_dev(sign)[1]
        )

    def accumulate(call, k):
        hz = hm[k]
        for b in range(bpp):
            qacc[...] += nt_dot(hz[:, b * LANE : (b + 1) * LANE], gath[call, k, b])

    def gather_ring(call, multiply, hook_first, hook_middle):
        copy = functools.partial(gather_copy, call)

        def step(ci, chain, s, first):
            if first is not True:
                if s - 1 < chain[3] if isinstance(s, int) else True:
                    copy(ci, chain, s - 1).wait_recv()
            if first is not None:
                copy(ci, chain, s).start()

        def after_step(s):
            if not multiply:
                send_batch(s)
                return
            if isinstance(s, int) and s == 0:
                qacc[...] = jnp.zeros((rows, samples), F32)
                accumulate(call, z)
                return
            accumulate(call, rotate(-s))
            accumulate(call, rotate(s))

        ring(step, after_step, hook_first, hook_middle)
        for ci, chain in enumerate(chains):
            if chain[3] == steps:
                copy(ci, chain, steps - 1).wait_recv()
            elif chain[3] == 0:
                pass
        if multiply:
            accumulate(call, rotate(steps))

    def reduce_copy(call, ci, chain, s):
        return remote(
            fsend.at[call, ci, s],
            frecv.at[call, ci, s],
            ring_sem.at[2 + call, 0, ci, s],
            ring_sem.at[2 + call, 1, ci, s],
            z_dev(chain[2])[1],
        )

    def reduce_ring(call, hook_first, hook_middle):
        copy = functools.partial(reduce_copy, call)
        wait_bytes(vb.at[call, pl.ds(0, n_plane - 1)], v_sem.at[call, 1])
        vector = vb[call].astype(F32).reshape(rows, samples).astype(BF16)

        def project(k):
            product = tn_dot(vector, hm[k])
            for b in range(bpp):
                fpart[k, b] = product[:, b * LANE : (b + 1) * LANE]

        for k in sorted({rotation % n_z for rotation in (steps, steps - 1, 1 - steps)}):
            project(rotate(k))

        def step(ci, chain, s, first):
            half, part, sign, count = chain
            if first is None:
                return
            target = rotate(sign * (count - s))
            value = fpart[target, pl.ds(half * hb, hb), pl.ds(part * sub, sub)]
            if first is not True:
                copy(ci, chain, s - 1).wait_recv()
                value = value + frecv[call, ci, s - 1].astype(F32)
            fsend[call, ci, s] = value.astype(BF16)
            copy(ci, chain, s).start()

        def after_step(s):
            if isinstance(s, int) and steps - 2 - s < 0:
                return
            if isinstance(s, int) and steps - 2 - s == 0:
                project(z)
                return
            project(rotate(steps - 2 - s))
            project(rotate(s + 2 - steps))

        ring(step, after_step, hook_first, hook_middle)
        for ci, chain in enumerate(chains):
            if chain[3] > 0:
                copy(ci, chain, chain[3] - 1).wait_recv()
        for half in range(2):
            for part in range(SPLIT):
                where = (z, pl.ds(half * hb, hb), pl.ds(part * sub, sub))
                total = fpart[where]
                for ci, chain in enumerate(chains):
                    if chain[:2] == (half, part) and chain[3] > 0:
                        total = total + frecv[call, ci, chain[3] - 1].astype(F32)
                fown[call, pl.ds(half * hb, hb), pl.ds(part * sub, sub)] = total.astype(BF16)

    def forward_sum(call):
        qp[call] = qacc[...].reshape(n_plane, OWN, samples)

        def send(k, c):
            p, _, _, dev = plane_dev(k)
            remote(
                qp.at[call, p], qr.at[call, me], q_sem.at[call, 0], q_sem.at[call, 1], dev
            ).start()
            return c

        lax.fori_loop(1, n_plane, send, 0)
        qr[call, me] = qp[call, me]
        wait_bytes(qr.at[call, pl.ds(0, n_plane - 1)], q_sem.at[call, 1])
        return jnp.sum(qr[call], axis=0)

    def share_start(call, value):
        vown[call] = value.astype(BF16)
        vb[call, me] = value.astype(BF16)

        def send(k, c):
            dev = plane_dev(k)[3]
            remote(
                vown.at[call], vb.at[call, me], v_sem.at[call, 0], v_sem.at[call, 1], dev
            ).start()
            return c

        lax.fori_loop(1, n_plane, send, 0)

    def spread_field(call):
        @pl.when(cell == 0)
        def _():
            fpad[call, pl.ds(0, REACH)] = jnp.zeros((REACH, s_rows, LANE), BF16)

        @pl.when(cell == n_cell - 1)
        def _():
            fpad[call, pl.ds(REACH + n_blocks, REACH)] = jnp.zeros((REACH, s_rows, LANE), BF16)

        def part(r):
            return fown.at[call, :, pl.ds(pl.multiple_of(r * s_rows, s_rows), s_rows)]

        def send(k, c):
            r = lax.rem(xc + k, n_r)
            remote(
                part(r),
                fpad.at[call, pl.ds(REACH + xc * bpp, bpp)],
                f_sem.at[call, 0],
                f_sem.at[call, 1],
                (r, cell),
            ).start()
            return c

        lax.fori_loop(1, n_r, send, 0)
        low = xc < n_half

        @pl.when(low & (cell > 0))
        def _():
            def send_low(k, c):
                r = lax.rem(xc + k, n_r)
                remote(
                    part(r),
                    fpad.at[call, pl.ds(REACH + n_blocks + xc * bpp, bpp)],
                    f_sem.at[call, 2],
                    f_sem.at[call, 3],
                    (r, cell - 1),
                ).start()
                return c

            lax.fori_loop(0, n_r, send_low, 0)

        @pl.when((xc >= n_r - n_half) & (cell < n_cell - 1))
        def _():
            def send_high(k, c):
                r = lax.rem(xc + k, n_r)
                remote(
                    part(r),
                    fpad.at[call, pl.ds((xc - (n_r - n_half)) * bpp, bpp)],
                    f_sem.at[call, 4],
                    f_sem.at[call, 5],
                    (r, cell + 1),
                ).start()
                return c

            lax.fori_loop(0, n_r, send_high, 0)

        own = pltpu.make_async_copy(
            part(xc), fpad.at[call, pl.ds(REACH + xc * bpp, bpp)], loc_sem.at[2 + bpp + call]
        )
        own.start()
        own.wait()
        body = fpad.at[call, pl.ds(0, (n_r - 1) * bpp)]
        halo = fpad.at[call, pl.ds(0, REACH)]
        wait_bytes(body, f_sem.at[call, 1])

        @pl.when(cell < n_cell - 1)
        def _():
            wait_bytes(halo, f_sem.at[call, 3])

        @pl.when(cell > 0)
        def _():
            wait_bytes(halo, f_sem.at[call, 5])

    def drain_spread(call):
        body = fpad.at[call, pl.ds(0, (n_r - 1) * bpp)]
        wide = fpad.at[call, pl.ds(0, n_blocks)]
        wait_bytes(body, f_sem.at[call, 0])

        @pl.when((xc < n_half) & (cell > 0))
        def _():
            wait_bytes(wide, f_sem.at[call, 2])

        @pl.when((xc >= n_r - n_half) & (cell < n_cell - 1))
        def _():
            wait_bytes(wide, f_sem.at[call, 4])

    def split(matrix):
        high = matrix.astype(BF16)
        return high, (matrix - high.astype(F32)).astype(BF16)

    def prior_apply(call):
        flat = (n_blocks * s_rows, LANE)
        high, low = split(center_ref[...])
        here = fpad[call, pl.ds(REACH, n_blocks)].reshape(flat)
        acc = nn_dot(here, high) + nn_dot(here, low)
        for band in range(bands_ref.shape[0]):
            offset = offsets_ref[band]
            high, low = split(bands_ref[band])
            ahead = fpad[call, pl.ds(REACH + offset, n_blocks)].reshape(flat)
            acc = acc + nn_dot(ahead, high) + nn_dot(ahead, low)
            behind = fpad[call, pl.ds(REACH - offset, n_blocks)].reshape(flat)
            acc = acc + nt_dot(behind, high) + nt_dot(behind, low)
        smooth[call] = acc.reshape(n_blocks, s_rows, LANE)

    row_id = lax.broadcasted_iota(jnp.int32, (s_rows, samples), 0)
    lane_id = lax.broadcasted_iota(jnp.int32, (s_rows, samples), 1)
    own_lane = lane_id == row_id + xc * s_rows

    def to_lanes(column):
        return jnp.sum(jnp.where(own_lane, column, 0.0), axis=0, keepdims=True)

    def to_column(lanes):
        return jnp.sum(jnp.where(own_lane, lanes, 0.0), axis=1, keepdims=True)

    def field_dot(field, image):
        return to_lanes(jnp.sum(jnp.sum(field * image, axis=0), axis=1, keepdims=True))

    def row_dot(a, b):
        return jnp.sum(a * b, axis=0, keepdims=True)

    def total_start(call, first, second):
        gvec[call] = jnp.concatenate(
            [first, second, jnp.zeros((OWN - 2, samples), F32)], axis=0
        )

        def send(k, c):
            dev = plane_dev(k)[3]
            remote(
                gvec.at[call], gplane.at[call, me], gp_sem.at[call, 0], gp_sem.at[call, 1], dev
            ).start()
            return c

        lax.fori_loop(1, n_plane, send, 0)
        gplane[call, me] = gvec[call]

    def total_middle(call):
        wait_bytes(gplane.at[call, pl.ds(0, n_plane - 1)], gp_sem.at[call, 1])
        gsum[call] = jnp.sum(gplane[call], axis=0)

        def send(k, c):
            _, dev = z_dev(k)
            remote(
                gsum.at[call], gz.at[call, z], gz_sem.at[call, 0], gz_sem.at[call, 1], dev
            ).start()
            return c

        lax.fori_loop(1, n_z, send, 0)
        gz[call, z] = gsum[call]

    def total_end(call):
        wait_bytes(gz.at[call, pl.ds(0, n_z - 1)], gz_sem.at[call, 1])
        total = jnp.sum(gz[call], axis=0)
        return total[0:1], total[1:2]

    def nothing():
        pass

    gather_ring(0, False, nothing, nothing)
    for load in loads:
        load.wait()
    shape = (OWN, observed_ref.shape[1])
    pick = lax.broadcasted_iota(jnp.int32, shape, 1) == lax.broadcasted_iota(
        jnp.int32, shape, 0
    ) + OWN * lax.rem(cell, observed_ref.shape[1] // OWN)
    line = pl.ds(lax.div(cell, observed_ref.shape[1] // OWN), 1)
    own_observed = jnp.sum(jnp.where(pick, observed_ref[line, :], 0.0), axis=1, keepdims=True)
    own_batch = jnp.sum(jnp.where(pick, batch_ref[line, :], 0), axis=1, keepdims=True)
    levels = (OWN, variance_ref.shape[1])
    noise_var = jnp.sum(
        jnp.where(lax.broadcasted_iota(jnp.int32, levels, 1) == own_batch, variance_ref[...], 0.0),
        axis=1,
        keepdims=True,
    )
    target = own_observed + jnp.sqrt(noise_var) * noise_ref[...]
    local_h.wait()
    wait_bytes(hbuf.at[:, pl.ds(0, n_plane - 1)], h_sem.at[1])
    qacc[...] = jnp.zeros((rows, samples), F32)

    def relayout(k, c):
        hm[k] = hbuf[k].astype(F32).reshape(rows, bpp * LANE).astype(BF16)
        accumulate(0, k)
        return c

    lax.fori_loop(0, n_z, relayout, 0)

    first = target - forward_sum(0)
    resid[0] = first
    share_start(0, first)
    reduce_ring(0, nothing, nothing)
    spread_field(0)
    prior_apply(0)

    sbf[...] = smooth[0].astype(BF16)

    def smooth_dst():
        return gath.at[1, z, :, pl.ds(pl.multiple_of(xc * s_rows, s_rows), s_rows)]

    def send_smooth(k, c):
        r = lax.rem(xc + k, n_r)
        remote(
            sbf.at[pl.ds(r * bpp, bpp)], smooth_dst(), s_sem.at[0], s_sem.at[1], (r, cell)
        ).start()
        return c

    lax.fori_loop(1, n_r, send_smooth, 0)
    keep = pltpu.make_async_copy(sbf.at[pl.ds(xc * bpp, bpp)], smooth_dst(), loc_sem.at[4 + bpp])
    keep.start()
    keep.wait()
    others = sbf.at[pl.ds(0, (n_r - 1) * bpp)]
    wait_bytes(others, s_sem.at[1])

    def start_first():
        r0 = resid[0]
        energy = field_dot(fpad[0, pl.ds(REACH, n_blocks)].astype(F32), smooth[0])
        total_start(0, row_dot(r0, r0), energy + row_dot(r0 * noise_var, r0))

    gather_ring(1, True, start_first, lambda: total_middle(0))
    applied = forward_sum(1) + noise_var * resid[0]
    norm0, curve0 = total_end(0)
    alpha0 = norm0 / curve0
    second = resid[0] - alpha0 * applied
    resid[1] = second
    share_start(1, second)

    def start_second():
        r1 = resid[1]
        total_start(1, row_dot(r1, r1), jnp.zeros((1, samples), F32))

    reduce_ring(1, start_second, lambda: total_middle(1))
    spread_field(1)
    prior_apply(1)
    norm1, _ = total_end(1)
    beta = norm1 / norm0
    direction = resid[1] + beta * resid[0]
    beta_column = to_column(beta)
    field0 = fpad[0, pl.ds(REACH, n_blocks)].astype(F32)
    field1 = fpad[1, pl.ds(REACH, n_blocks)].astype(F32)
    energy = field_dot(field1 + beta_column * field0, smooth[1] + beta_column * smooth[0])
    total_start(2, energy + row_dot(direction * noise_var, direction), jnp.zeros((1, samples), F32))
    for call in range(2):
        drain(functools.partial(gather_copy, call))
        drain(functools.partial(reduce_copy, call))
        drain_spread(call)
        wait_bytes(qp.at[call, pl.ds(0, n_plane - 1)], q_sem.at[call, 0])
        wait_bytes(vb.at[call, pl.ds(0, n_plane - 1)], v_sem.at[call, 0])
        wait_bytes(gplane.at[call, pl.ds(0, n_plane - 1)], gp_sem.at[call, 0])
        wait_bytes(gz.at[call, pl.ds(0, n_z - 1)], gz_sem.at[call, 0])
    wait_bytes(others, s_sem.at[0])
    wait_bytes(hbuf.at[:, pl.ds(0, n_plane - 1)], h_sem.at[0])
    local_p.wait()
    total_middle(2)
    curve1, _ = total_end(2)
    alpha1 = norm1 / curve1
    weights_ref[...] = alpha0 * resid[0] + alpha1 * direction
    scale0 = to_column(alpha0 + alpha1 * beta)
    scale1 = to_column(alpha1)
    for b in range(n_blocks):
        columns = slice(b * LANE, (b + 1) * LANE)
        post_ref[:, columns] = (
            own_prior[:, columns].astype(F32) + scale0 * smooth[0, b] + scale1 * smooth[1, b]
        )
    wait_bytes(gplane.at[2, pl.ds(0, n_plane - 1)], gp_sem.at[2, 0])
    wait_bytes(gz.at[2, pl.ds(0, n_z - 1)], gz_sem.at[2, 0])


def local(
    n_r,
    n_z,
    n_y,
    n_low,
    footprint,
    prior_draws,
    observed,
    obs_noise,
    batch_of,
    batch_variance,
    band_offsets,
    center_block,
    band_blocks,
):
    samples = obs_noise.shape[1]
    n_blocks = prior_draws.shape[1] // LANE
    bpp = n_blocks // n_r
    n_plane = n_r * n_y * n_low
    s_rows = samples // n_r
    width = bpp * LANE
    rows = n_plane * OWN
    hb = bpp // 2
    steps = n_z // 2
    tiles = footprint.reshape(OWN, n_z, n_y * n_low, n_r, width).transpose(1, 2, 3, 0, 4)
    count = observed.shape[0]
    lines = (max(count // LANE, 1), min(count, LANE))
    observed = observed.reshape(lines)
    batch_of = batch_of.reshape(lines)
    batch_variance = batch_variance.reshape(1, batch_variance.shape[0])
    vmem = pl.BlockSpec(memory_space=pltpu.VMEM)
    hbm = pl.BlockSpec(memory_space=pl.ANY)
    dma = pltpu.SemaphoreType.DMA
    return pl.pallas_call(
        functools.partial(kernel, (n_r, n_z, n_y, n_low, bpp, samples)),
        out_shape=(
            jax.ShapeDtypeStruct((s_rows, n_blocks * LANE), F32),
            jax.ShapeDtypeStruct((OWN, samples), F32),
        ),
        in_specs=[hbm] * 6 + [pl.BlockSpec(memory_space=pltpu.SMEM), hbm, hbm],
        out_specs=(vmem, vmem),
        scratch_shapes=[
            pltpu.VMEM((n_z, n_plane, OWN, width), BF16),
            pltpu.VMEM((n_z, rows, width), BF16),
            pltpu.VMEM((2, n_z, bpp, samples, LANE), BF16),
            pltpu.VMEM((s_rows, n_blocks * LANE), BF16),
            pltpu.VMEM((2, n_plane, OWN, samples), F32),
            pltpu.VMEM((2, n_plane, OWN, samples), F32),
            pltpu.VMEM((2, OWN, samples), BF16),
            pltpu.VMEM((2, n_plane, OWN, samples), BF16),
            pltpu.VMEM((n_z, bpp, samples, LANE), F32),
            pltpu.VMEM((2, 4 * SPLIT, steps, hb, samples // SPLIT, LANE), BF16),
            pltpu.VMEM((2, 4 * SPLIT, steps, hb, samples // SPLIT, LANE), BF16),
            pltpu.VMEM((2, bpp, samples, LANE), BF16),
            pltpu.VMEM((2, n_blocks + 2 * REACH, s_rows, LANE), BF16),
            pltpu.VMEM((2, n_blocks, s_rows, LANE), F32),
            pltpu.VMEM((n_blocks, s_rows, LANE), BF16),
            pltpu.VMEM((2, OWN, samples), F32),
            pltpu.VMEM((3, OWN, samples), F32),
            pltpu.VMEM((3, n_plane, OWN, samples), F32),
            pltpu.VMEM((3, OWN, samples), F32),
            pltpu.VMEM((3, n_z, OWN, samples), F32),
            pltpu.VMEM((rows, samples), F32),
            pltpu.VMEM(observed.shape, F32),
            pltpu.VMEM((OWN, samples), F32),
            pltpu.VMEM(batch_of.shape, jnp.int32),
            pltpu.VMEM(batch_variance.shape, F32),
            pltpu.VMEM(center_block.shape, F32),
            pltpu.VMEM(band_blocks.shape, F32),
            dma((2,)),
            dma((2, 2)),
            dma((2, 2)),
            dma((4, 2, 4 * SPLIT, steps)),
            dma((2, 6)),
            dma((2,)),
            dma((3, 2)),
            dma((3, 2)),
            dma((11 + bpp,)),
        ],
        compiler_params=pltpu.CompilerParams(
            collective_id=0, has_side_effects=True, vmem_limit_bytes=56 * 1024 * 1024
        ),
    )(
        tiles,
        prior_draws,
        observed,
        obs_noise,
        batch_of,
        batch_variance,
        band_offsets,
        center_block,
        band_blocks,
    )


def solution(mesh, n_y=4):
    n_r = mesh.shape["rcpt"]
    n_z = mesh.shape["cell"] // (n_y * LOW)
    return jax.shard_map(
        functools.partial(local, n_r, n_z, n_y, LOW),
        mesh=mesh,
        in_specs=(
            P(("rcpt", "cell"), None),
            P(None, "cell"),
            P("rcpt"),
            P("rcpt", None),
            P("rcpt"),
            P(),
            P(),
            P(),
            P(),
        ),
        out_specs=(P("rcpt", "cell"), P(("rcpt", "cell"), None)),
        check_vma=False,
    )
```

time: 204 us -> 177 us (0.87)
  Pallas kernels: 196 us -> 173 us
  other arithmetic: 2.19 us -> 0 us
  local copies, waits for them, and re-layouts: 5.01 us -> 2.85 us
    pallas_call x1, Pallas kernels: 196 us -> 173 us  [local(): pl.pallas_call(functools.partial(kernel, (n_r, n_z, n_y, n_low, bpp, samp...]
where the time goes in v2:
time: 177 us
  Pallas kernels  173 us (98%)
  local copies, waits for them, and re-layouts  2.85 us (2%)
    pallas_call x1, Pallas kernels, local(): pl.pallas_call(functools.partial(kernel, (n_r, n_z, n_y, n_low, bpp, samp...  173 us

profile of v2, /device:TPU:1, one launch (start us, length us, event | category | flops | bytes accessed | tf_op | source)
XLA Modules:
  0.0 176.9 jit_solution(1702365565806084131)
XLA Ops:
  0.6 173.4 %shard_map.104 = (f32[16,2048]{1,0:T(8,128)}, f32[8,128]{1,0:T(8,128)}) custom-call(bf16[8,8,8,8,256]{4,3,2,1,0:T(8,128)(2,1)} %bitcast.6, bf16[128,2048]{1,0:T(8,128)(2,1)} %prior_ref.1, f32[4,128]{1,0:T(4,128)} %bitcast.7, f32[512,128]{1,0:T(8,128)} %noise_hbm.1, s32[4,128]{1,0:T(4,128)} %bitcast.8, f32[1,64]{1,0:T(1,128)} %bitcast.9, s32[3]{0:T(128)} %offsets_ref.1, ...), custom_call_target="tpu_custom_call" | custom-call | tf_op jit(solution)/shard_map/pallas_call | solution.py:688
  174.1 1.6 copy.13
  175.7 1.3 copy.14

commit v3 on v2

--- a/solution.py
+++ b/solution.py
@@ -95,10 +95,20 @@
     within = lax.rem(cell, near)
     me = xc * near + within
 
-    def plane_dev(i):
+    height = lax.div(cell, n_y)
+    level = lax.div(within, n_y)
+    kind = lax.rem(xc, 2)
+
+    def paired(xx, low, way):
+        away = lax.rem(lax.div(low, n_y) + n_low - level, n_low)
+        there = height + away * (1 - 2 * level) * (1 - 2 * way)
+        there = lax.rem(there + n_z * n_low, n_z * n_low)
+        return (xx, there * n_y + lax.rem(low, n_y))
+
+    def plane_dev(i, way=None):
         p = lax.rem(me + i * STRIDE, n_plane)
         xx, low = lax.div(p, near), lax.rem(p, near)
-        return p, xx, low, (xx, z * near + low)
+        return p, xx, low, paired(xx, low, lax.rem(xx, 2) if way is None else way)
 
     def z_dev(k):
         zz = lax.rem(z + k + n_z, n_z)
@@ -127,53 +137,36 @@
 
     barrier = pltpu.get_barrier_semaphore()
 
-    def greet_plane(k, c):
-        pl.semaphore_signal(barrier, inc=1, device_id=plane_dev(k)[3], device_id_type=MESH)
-        return c
-
-    lax.fori_loop(1, n_plane, greet_plane, 0)
-
+    flat = n_r * n_y
+    mine = xc * n_y + lax.rem(within, n_y)
+
+    def greet(rise):
+        def body(i, c):
+            t = lax.rem(mine + i, flat)
+            there = lax.rem(height + rise + n_z * n_low, n_z * n_low)
+            dev = (lax.div(t, n_y), there * n_y + lax.rem(t, n_y))
+            pl.semaphore_signal(barrier, inc=1, device_id=dev, device_id_type=MESH)
+            return c
+
+        return body
+
+    lax.fori_loop(1, flat, greet(0), 0)
+    lax.fori_loop(0, flat, greet(1), 0)
+    lax.fori_loop(0, flat, greet(-1), 0)
     for sign in (1, -1):
         pl.semaphore_signal(barrier, inc=1, device_id=z_dev(sign)[1], device_id_type=MESH)
-    edge_lo = (within == 0) & (z > 0)
-    edge_hi = (within == near - 1) & (z < n_z - 1)
-
-    @pl.when(edge_lo)
-    def _():
-        def greet(k, c):
-            pl.semaphore_signal(barrier, inc=1, device_id=(k, cell - 1), device_id_type=MESH)
-            return c
-
-        lax.fori_loop(0, n_r, greet, 0)
-
-    @pl.when(edge_hi)
-    def _():
-        def greet(k, c):
-            pl.semaphore_signal(barrier, inc=1, device_id=(k, cell + 1), device_id_type=MESH)
-            return c
-
-        lax.fori_loop(0, n_r, greet, 0)
-
-    greeted = n_plane - 1 + 2
-
-    @pl.when(edge_lo | edge_hi)
-    def _():
-        pl.semaphore_wait(barrier, greeted + n_r)
-
-    @pl.when(jnp.logical_not(edge_lo | edge_hi))
-    def _():
-        pl.semaphore_wait(barrier, greeted)
-
-    flat = n_r * n_y
-    level = lax.div(within, n_y)
-    mine = xc * n_y + lax.rem(within, n_y)
+    pl.semaphore_wait(barrier, 3 * flat - 1 + 2)
 
     def send_h(i, hop):
         t = lax.rem(mine + i * STRIDE, flat)
         xx = lax.div(t, n_y)
         low = lax.rem(level + hop, n_low) * n_y + lax.rem(t, n_y)
         remote(
-            h_ref.at[:, low, xx], hbuf.at[:, me], h_sem.at[0], h_sem.at[1], (xx, z * near + low)
+            h_ref.at[:, low, xx],
+            hbuf.at[:, me],
+            h_sem.at[0],
+            h_sem.at[1],
+            paired(xx, low, lax.rem(xx, 2)),
         ).start()
 
     def send_same(i, c):
@@ -363,7 +356,7 @@
         qp[call] = qacc[...].reshape(n_plane, OWN, samples)
 
         def send(k, c):
-            p, _, _, dev = plane_dev(k)
+            p, _, _, dev = plane_dev(k, kind)
             remote(
                 qp.at[call, p], qr.at[call, me], q_sem.at[call, 0], q_sem.at[call, 1], dev
             ).start()
@@ -513,7 +506,7 @@
         )
 
         def send(k, c):
-            dev = plane_dev(k)[3]
+            dev = plane_dev(k, 0)[3]
             remote(
                 gvec.at[call], gplane.at[call, me], gp_sem.at[call, 0], gp_sem.at[call, 1], dev
             ).start()

time: 177 us -> 171 us (0.966)
  Pallas kernels: 173 us -> 168 us
    pallas_call x1, Pallas kernels: 173 us -> 168 us  [local(): pl.pallas_call(functools.partial(kernel, (n_r, n_z, n_y, n_low, bpp, samp...]
where the time goes in v3:
time: 171 us
  Pallas kernels  168 us (98%)
  local copies, waits for them, and re-layouts  2.85 us (2%)
    pallas_call x1, Pallas kernels, local(): pl.pallas_call(functools.partial(kernel, (n_r, n_z, n_y, n_low, bpp, samp...  168 us

profile of v3, /device:TPU:1, one launch (start us, length us, event | category | flops | bytes accessed | tf_op | source)
XLA Modules:
  0.0 171.1 jit_solution(15495478840989095400)
XLA Ops:
  0.6 167.6 %shard_map.104 = (f32[16,2048]{1,0:T(8,128)}, f32[8,128]{1,0:T(8,128)}) custom-call(bf16[8,8,8,8,256]{4,3,2,1,0:T(8,128)(2,1)} %bitcast.6, bf16[128,2048]{1,0:T(8,128)(2,1)} %prior_ref.1, f32[4,128]{1,0:T(4,128)} %bitcast.7, f32[512,128]{1,0:T(8,128)} %noise_hbm.1, s32[4,128]{1,0:T(4,128)} %bitcast.8, f32[1,64]{1,0:T(1,128)} %bitcast.9, s32[3]{0:T(128)} %offsets_ref.1, ...), custom_call_target="tpu_custom_call" | custom-call | tf_op jit(solution)/shard_map/pallas_call | solution.py:681
  168.3 1.6 copy.13
  169.8 1.3 copy.14

commit v4 on v3

--- a/solution.py
+++ b/solution.py
@@ -176,12 +176,12 @@
     lax.fori_loop(1, flat, send_same, 0)
     batch = flat * (n_low - 1) // (n_z // 2)
 
-    def send_batch(s):
+    def send_batch(first, last):
         def body(i, c):
             send_h(lax.rem(i, flat), 1 + lax.div(i, flat))
             return c
 
-        lax.fori_loop(s * batch, (s + 1) * batch, body, 0)
+        lax.fori_loop(first * batch, last * batch, body, 0)
 
     local_h.start()
     local_p.start()
@@ -278,7 +278,10 @@
 
         def after_step(s):
             if not multiply:
-                send_batch(s)
+                if isinstance(s, int) and s == 0:
+                    send_batch(0, 2)
+                elif not (isinstance(s, int) and s == steps - 1):
+                    send_batch(s + 1, s + 2)
                 return
             if isinstance(s, int) and s == 0:
                 qacc[...] = jnp.zeros((rows, samples), F32)

time: 171 us -> 171 us (level)
  no operation moved by 1% of the time
where the time goes in v4:
time: 171 us
  Pallas kernels  167 us (98%)
  local copies, waits for them, and re-layouts  2.85 us (2%)
    pallas_call x1, Pallas kernels, local(): pl.pallas_call(functools.partial(kernel, (n_r, n_z, n_y, n_low, bpp, samp...  167 us

profile of v4, /device:TPU:1, one launch (start us, length us, event | category | flops | bytes accessed | tf_op | source)
XLA Modules:
  0.0 170.5 jit_solution(17006773279306725089)
XLA Ops:
  0.6 167.0 %shard_map.104 = (f32[16,2048]{1,0:T(8,128)}, f32[8,128]{1,0:T(8,128)}) custom-call(bf16[8,8,8,8,256]{4,3,2,1,0:T(8,128)(2,1)} %bitcast.6, bf16[128,2048]{1,0:T(8,128)(2,1)} %prior_ref.1, f32[4,128]{1,0:T(4,128)} %bitcast.7, f32[512,128]{1,0:T(8,128)} %noise_hbm.1, s32[4,128]{1,0:T(4,128)} %bitcast.8, f32[1,64]{1,0:T(1,128)} %bitcast.9, s32[3]{0:T(128)} %offsets_ref.1, ...), custom_call_target="tpu_custom_call" | custom-call | tf_op jit(solution)/shard_map/pallas_call | solution.py:684
  167.7 1.6 copy.13
  169.2 1.3 copy.14
